TPU v7x, 256 devices: a whole 4x4x8 slice. The times are simulated.
256 devices in a mesh: dp: 8 (over z_hi, x), expert: 32 (over z_lo, y, core).
Axes of the slice: x: 4, y: 4, z: 8 (z_hi: 2, z_lo: 4; z = z_hi * 4 + z_lo), core: 2. Of those that a mesh axis runs over, the one named last changes fastest.
Arguments:
- tokens: bfloat16 [32768, 3584], P(('dp', 'expert')), may hold values from -6 to 6
- cotangent: bfloat16 [32768, 3584], P(('dp', 'expert')), may hold values from -0.09375 to 0.09375
- expert_ids: int32 [32768, 8], P(('dp', 'expert')), may hold values from 0 to 255, all different within a row; in each aligned block of 128 rows (0 to 127, 128 to 255, ...) at most 6 rows name the same one
- gates: bfloat16 [32768, 8], P(('dp', 'expert')), may hold values from 0.049804688 to 1
- swap_flags: int32 [16], replicated, may hold values 0 or 1
- gate_w: bfloat16 [32, 3584, 1024], P('expert', None, 'dp'), may hold values from -0.09375 to 0.09375
- up_w: bfloat16 [32, 3584, 1024], P('expert', None, 'dp'), may hold values from -0.09375 to 0.09375
- down_w: bfloat16 [32, 1024, 3584], P('expert', 'dp'), may hold values from -0.1875 to 0.1875
Outputs:
- grad_gate_w: bfloat16 [32, 3584, 1024], P('expert', None, 'dp')
- grad_up_w: bfloat16 [32, 3584, 1024], P('expert', None, 'dp')
- grad_down_w: bfloat16 [32, 1024, 3584], P('expert', 'dp')
- score_grad: float32 [32768, 8], P(('dp', 'expert'))
Inputs may be any that keep to these rules, and one draw needn't show every extreme that they name: `expert_ids`: among the 128 rows of one device no expert is named more than 6 times, a bound that some block reaches; the numbers of one row differ. `swap_flags`: 1 means that slots s and s + 16 trade their experts.
All inputs are finite; a program needn't handle non-finite values.
Results may differ from a plain program's by a relative error of at most 0.011.
Values may be sent and summed in bfloat16 or wider, within the bound.
A program may use at most 128 MiB of HBM per device.

v0:
```python
import functools

import jax
import jax.numpy as jnp
from jax import lax
from jax.experimental import pallas as pl
from jax.experimental.pallas import tpu as pltpu
from jax.sharding import PartitionSpec as P

CAP = 6
LANE = 128


def dp_gather_kernel(n_dp, ring, chunks, n_ex, x_ref, wg_ref, wu_ref, wd_ref, o_ref, og_ref, ou_ref, od_ref, recv, recv_z, recv_w, send):
    me = lax.axis_index("dp")
    ex = lax.axis_index("expert")
    rows = x_ref.shape[1]
    half = rows // 2
    piece = rows // chunks
    plane = me // ring
    pos = me % ring
    left = plane * ring + (pos + ring - 1) % ring
    right = plane * ring + (pos + 1) % ring
    far = plane * ring + (pos + 2) % ring
    across = (me + ring) % n_dp
    twin = (ex + n_ex // 2) % n_ex

    def span(k, start, size):
        return o_ref.at[:, pl.ds(k * rows + start, size), :]

    def push(src, dst, slot, sem, peer):
        copy = pltpu.make_async_remote_copy(
            src_ref=src,
            dst_ref=dst,
            send_sem=send.at[slot],
            recv_sem=sem,
            device_id=(peer, ex),
            device_id_type=pl.DeviceIdType.MESH,
        )
        copy.start()
        return copy

    def arrived(ref, sem):
        pltpu.make_async_copy(ref, ref, sem).wait()

    barrier = pltpu.get_barrier_semaphore()
    for peer in (left, right, across):
        pl.semaphore_signal(barrier, inc=1, device_id=(peer, ex), device_id_type=pl.DeviceIdType.MESH)
    pl.semaphore_signal(barrier, inc=1, device_id=(me, twin), device_id_type=pl.DeviceIdType.MESH)
    pl.semaphore_wait(barrier, 4)

    local = pltpu.make_async_copy(x_ref, span(me, 0, rows), recv.at[me])
    local.start()
    swaps = []
    for index, (src, dst) in enumerate(((wg_ref, og_ref), (wu_ref, ou_ref), (wd_ref, od_ref))):
        copy = pltpu.make_async_remote_copy(
            src_ref=src,
            dst_ref=dst,
            send_sem=send.at[3 * chunks + 6 + index],
            recv_sem=recv_w.at[index],
            device_id=(me, twin),
            device_id_type=pl.DeviceIdType.MESH,
        )
        copy.start()
        swaps.append(copy)
    sent = []
    for q in range(chunks):
        sent.append(
            push(
                x_ref.at[:, pl.ds(q * piece, piece), :],
                span(me, q * piece, piece),
                len(sent),
                recv_z.at[q],
                across,
            )
        )
    sent.append(push(x_ref, span(me, 0, rows), len(sent), recv.at[me], left))
    sent.append(push(x_ref, span(me, 0, rows), len(sent), recv.at[me], right))
    arrived(span(left, 0, rows), recv.at[left])
    sent.append(push(span(left, 0, half), span(left, 0, half), len(sent), recv.at[left], right))
    arrived(span(right, 0, rows), recv.at[right])
    sent.append(push(span(right, half, half), span(right, half, half), len(sent), recv.at[right], left))
    for q in range(chunks):
        chunk = span(across, q * piece, piece)
        arrived(chunk, recv_z.at[q])
        sent.append(push(chunk, chunk, len(sent), recv.at[across], left))
        sent.append(push(chunk, chunk, len(sent), recv.at[across], right))
    left_across = (left + ring) % n_dp
    right_across = (right + ring) % n_dp
    arrived(span(left_across, 0, rows), recv.at[left_across])
    sent.append(
        push(span(left_across, 0, half), span(left_across, 0, half), len(sent), recv.at[left_across], right)
    )
    arrived(span(right_across, 0, rows), recv.at[right_across])
    sent.append(
        push(span(right_across, half, half), span(right_across, half, half), len(sent), recv.at[right_across], left)
    )
    arrived(span(far, 0, rows), recv.at[far])
    far_across = (far + ring) % n_dp
    arrived(span(far_across, 0, rows), recv.at[far_across])
    local.wait()
    for copy in sent:
        copy.wait_send()
    for copy in swaps:
        copy.wait()


def dp_gather(block, w_gate, w_up, w_down):
    n_dp = lax.axis_size("dp")
    n_ex = lax.axis_size("expert")
    ring = n_dp // 2
    chunks = 4
    cap, rows, row_width = block.shape
    sends = 3 * chunks + 6 + 3
    weights = (w_gate, w_up, w_down)
    return pl.pallas_call(
        functools.partial(dp_gather_kernel, n_dp, ring, chunks, n_ex),
        out_shape=(jax.ShapeDtypeStruct((cap, n_dp * rows, row_width), block.dtype),)
        + tuple(jax.ShapeDtypeStruct(w.shape, w.dtype) for w in weights),
        in_specs=[pl.BlockSpec(memory_space=pl.ANY)] * 4,
        out_specs=(pl.BlockSpec(memory_space=pl.ANY),) * 4,
        scratch_shapes=[
            pltpu.SemaphoreType.DMA((n_dp,)),
            pltpu.SemaphoreType.DMA((chunks,)),
            pltpu.SemaphoreType.DMA((3,)),
            pltpu.SemaphoreType.DMA((sends,)),
        ],
        compiler_params=pltpu.CompilerParams(collective_id=0, has_side_effects=True),
    )(block, w_gate, w_up, w_down)


def expert_exchange_kernel(n_ex, x_ref, o_ref, recv, send, local_sem):
    me = lax.axis_index("expert")
    dp = lax.axis_index("dp")
    barrier = pltpu.get_barrier_semaphore()
    for step in range(1, n_ex):
        peer = (me + step) % n_ex
        pl.semaphore_signal(barrier, inc=1, device_id=(dp, peer), device_id_type=pl.DeviceIdType.MESH)
    pl.semaphore_wait(barrier, n_ex - 1)
    local = pltpu.make_async_copy(x_ref.at[pl.ds(me, 1)], o_ref.at[pl.ds(me, 1)], local_sem.at[0])
    local.start()
    sent = []
    for step in range(1, n_ex):
        peer = (me + step) % n_ex
        copy = pltpu.make_async_remote_copy(
            src_ref=x_ref.at[pl.ds(peer, 1)],
            dst_ref=o_ref.at[pl.ds(me, 1)],
            send_sem=send.at[step],
            recv_sem=recv.at[0],
            device_id=(dp, peer),
            device_id_type=pl.DeviceIdType.MESH,
        )
        copy.start()
        sent.append(copy)
    pltpu.make_async_copy(
        x_ref.at[pl.ds(0, n_ex - 1)], o_ref.at[pl.ds(0, n_ex - 1)], recv.at[0]
    ).wait()
    local.wait()
    for copy in sent:
        copy.wait_send()


def expert_exchange(block):
    n_ex = lax.axis_size("expert")
    return pl.pallas_call(
        functools.partial(expert_exchange_kernel, n_ex),
        out_shape=jax.ShapeDtypeStruct(block.shape, block.dtype),
        in_specs=[pl.BlockSpec(memory_space=pl.ANY)],
        out_specs=pl.BlockSpec(memory_space=pl.ANY),
        scratch_shapes=[
            pltpu.SemaphoreType.DMA((1,)),
            pltpu.SemaphoreType.DMA((n_ex,)),
            pltpu.SemaphoreType.DMA((1,)),
        ],
        compiler_params=pltpu.CompilerParams(collective_id=1, has_side_effects=True),
    )(block)


def body(tokens, cotangent, expert_ids, gates, swap_flags, gate_w, up_w, down_w):
    axis_len = lax.axis_size("expert")
    half_axis = axis_len // 2
    own_slot = lax.axis_index("expert")
    tok_count = tokens.shape[0]
    top_count = expert_ids.shape[1]
    width = tokens.shape[1]
    flat_ids = expert_ids.reshape(-1)
    choice_count = flat_ids.shape[0]
    valid = flat_ids < axis_len
    pair_index = jnp.arange(half_axis, dtype=jnp.int32)
    flag_of = jnp.sum(
        jnp.where((flat_ids % half_axis)[:, None] == pair_index[None, :], swap_flags[None, :], 0),
        axis=1,
    )
    own_flag = jnp.sum(jnp.where(pair_index == own_slot % half_axis, swap_flags, 0))
    target = jnp.where(flag_of == 1, jnp.bitwise_xor(flat_ids, half_axis), flat_ids)
    target = jnp.where(valid, target, 0)
    onehot = (
        (target[:, None] == jnp.arange(axis_len, dtype=jnp.int32)[None, :]) & valid[:, None]
    ).astype(jnp.bfloat16)
    order = jnp.arange(choice_count, dtype=jnp.int32)
    lower = (order[None, :] <= order[:, None]).astype(jnp.bfloat16)
    counts = jnp.dot(lower, onehot, preferred_element_type=jnp.float32)
    ranks = jnp.sum(counts * onehot.astype(jnp.float32), axis=1).astype(jnp.int32) - 1
    slot_count = axis_len * CAP
    slots = jnp.where(valid, target * CAP + ranks, slot_count)
    pick = (slots[:, None] == jnp.arange(slot_count, dtype=jnp.int32)[None, :]).astype(jnp.bfloat16)
    token_pick = jnp.sum(pick.reshape(tok_count, top_count, slot_count).astype(jnp.float32), axis=1)
    token_pick = token_pick.astype(jnp.bfloat16)
    rows_xdy = lax.dot_general(
        token_pick,
        jnp.concatenate([tokens, cotangent], axis=1),
        (((0,), (0,)), ((), ())),
        preferred_element_type=jnp.float32,
    ).astype(tokens.dtype)
    send_g = jnp.dot(gates.reshape(1, -1), pick, preferred_element_type=jnp.float32).astype(gates.dtype)
    g_cols = jnp.where(
        jnp.arange(LANE, dtype=jnp.int32)[None, :] == 0, send_g.reshape(-1, 1), jnp.zeros((), gates.dtype)
    )
    packed = jnp.concatenate([rows_xdy, g_cols], axis=1)
    row_width = packed.shape[1]
    packed = packed.reshape(axis_len, CAP * row_width // LANE, LANE)
    recv = expert_exchange(packed).reshape(axis_len, CAP, row_width)
    recv = jnp.transpose(recv, (1, 0, 2))
    gathered, other_gate, other_up, other_down = dp_gather(recv, gate_w, up_w, down_w)
    taken = own_flag == 1
    w_gate = jnp.where(taken, other_gate[0], gate_w[0])
    w_up = jnp.where(taken, other_up[0], up_w[0])
    w_down = jnp.where(taken, other_down[0], down_w[0])
    block_count = lax.axis_size("dp")
    row_x = gathered[:, :, :width]
    row_dy = gathered[:, :, width:2 * width]
    row_g = gathered[:, :, 2 * width:2 * width + 1]
    feature = (((2,), (0,)), ((), ()))
    rows_contract = (((0, 1), (0, 1)), ((), ()))
    hidden_count = w_gate.shape[1]
    w_both = jnp.concatenate([w_gate, w_up], axis=1)
    pre_both = lax.dot_general(row_x, w_both, feature, preferred_element_type=jnp.float32)
    pre_gate = pre_both[:, :, :hidden_count]
    pre_up = pre_both[:, :, hidden_count:]
    sigma = jax.nn.sigmoid(pre_gate)
    active = pre_gate * sigma
    hidden = (active * pre_up).astype(jnp.bfloat16)
    back = lax.dot_general(
        row_dy, w_down, (((2,), (1,)), ((), ())), preferred_element_type=jnp.float32
    )
    score = jnp.sum(hidden.astype(jnp.float32) * back, axis=2).T
    scaled = row_dy * row_g
    d_hidden = row_g.astype(jnp.float32) * back
    d_gate = (d_hidden * pre_up * sigma * (1.0 + pre_gate * (1.0 - sigma))).astype(jnp.bfloat16)
    d_up = (d_hidden * active).astype(jnp.bfloat16)
    d_both = jnp.concatenate([d_gate, d_up], axis=2)
    grad_both = lax.dot_general(row_x, d_both, rows_contract, preferred_element_type=jnp.float32)
    grad_gate = grad_both[:, :hidden_count]
    grad_up = grad_both[:, hidden_count:]
    grad_down = lax.dot_general(hidden, scaled, rows_contract, preferred_element_type=jnp.float32)
    scores = score.reshape(block_count, axis_len * CAP)
    parts = lax.all_to_all(scores, "dp", split_axis=0, concat_axis=0, tiled=True)
    own_scores = jnp.sum(parts, axis=0).reshape(axis_len, CAP)
    returned = lax.all_to_all(own_scores, "expert", split_axis=0, concat_axis=0, tiled=True)
    picked = jnp.sum(jnp.where(pick > 0, returned.reshape(1, -1), 0.0), axis=1)
    score_grad = jnp.where(valid, picked, 0.0).reshape(tok_count, top_count)
    out_gate = grad_gate.astype(jnp.bfloat16)[None]
    out_up = grad_up.astype(jnp.bfloat16)[None]
    out_down = grad_down.astype(jnp.bfloat16)[None]
    return (out_gate, out_up, out_down, score_grad)


def solution(mesh):
    placed = (
        P(("dp", "expert"), None),
        P(("dp", "expert"), None),
        P(("dp", "expert"), None),
        P(("dp", "expert"), None),
        P(),
        P("expert", None, "dp"),
        P("expert", None, "dp"),
        P("expert", "dp", None),
    )
    return jax.shard_map(
        body,
        mesh=mesh,
        in_specs=placed,
        out_specs=(
            P("expert", None, "dp"),
            P("expert", None, "dp"),
            P("expert", "dp", None),
            P(("dp", "expert"), None),
        ),
        check_vma=False,
    )
```

profile of v0, /device:TPU:1, one launch (start us, length us, event | category | flops | bytes accessed | tf_op | source)
XLA Modules:
  0.0 400.1 jit_solution(10230696513910568123)
XLA Ops:
  0.7 0.8 copy.44
  1.6 0.8 copy.39
  2.5 0.7 select_reduce_fusion.1
  3.2 0.5 fusion.32
  4.5 2.3 convolution_convert_fusion
  7.0 4.5 %reshape.127.x_ref = bf16[32,342,128]{2,1,0:T(8,128)(2,1)} reshape(bf16[192,7296]{1,0:T(8,128)(2,1)S(1)} %pad_maximum_fusion) | data formatting | bytes 5603328 | tf_op jit(solution)/shard_map/reshape | solution.py:221
  11.5 60.9 %shard_map.111 = bf16[32,342,128]{2,1,0:T(8,128)(2,1)} custom-call(bf16[32,342,128]{2,1,0:T(8,128)(2,1)} %reshape.127.x_ref), custom_call_target="tpu_custom_call" | custom-call | tf_op jit(solution)/shard_map/pallas_call | solution.py:165
  72.5 6.3 %reshape.128 = bf16[32,6,7296]{2,1,0:T(8,128)(2,1)} reshape(bf16[32,342,128]{2,1,0:T(8,128)(2,1)} %shard_map.111) | data formatting | bytes 5603328 | tf_op jit(solution)/shard_map/reshape | solution.py:222
  78.8 3.9 copy.58
  82.7 0.6 fusion.56
  83.3 258.4 %shard_map.112 = (bf16[6,256,7296]{2,1,0:T(8,128)(2,1)}, bf16[1,3584,128]{2,1,0:T(8,128)(2,1)}, bf16[1,3584,128]{2,1,0:T(8,128)(2,1)}, bf16[1,128,3584]{2,1,0:T(8,128)(2,1)}) custom-call(bf16[6,32,7296]{2,1,0:T(8,128)(2,1)} %bitcast.38, bf16[1,3584,128]{2,1,0:T(8,128)(2,1)} %wg_ref.1, bf16[1,3584,128]{2,1,0:T(8,128)(2,1)} %wu_ref.1, bf16[1,128,3584]{2,1,0:T(8,128)(2,1)} %wd_ref.1), custom_call_target="tpu_custom_call" | custom-call | tf_op jit(solution)/shard_map/pallas_call | solution.py:116
  341.7 1.2 slice_reduce_fusion
  343.9 6.0 %fusion.7 = f32[6,256,256]{1,2,0:T(8,128)S(1)} fusion(bf16[6,256,7296]{2,1,0:T(8,128)(2,1)} %get-tuple-element.8, bf16[3584,128]{1,0:T(8,128)(2,1)S(1)} %get-tuple-element.37, bf16[3584,128]{1,0:T(8,128)(2,1)S(1)} %get-tuple-element.38), kind=kOutput, calls=%fused_computation.7 | convolution fusion | flops 2822242304 | bytes 14417920 | tf_op jit(solution)/shard_map/dot_general | solution.py:237
  350.0 7.9 %multiply_reduce_fusion = (f32[6,256]{1,0:T(8,128)S(1)}, bf16[6,256,128]{1,2,0:T(8,128)(2,1)S(1)}, bf16[6,256,128]{1,2,0:T(8,128)(2,1)S(1)}, bf16[6,256,128]{1,2,0:T(8,128)(2,1)S(1)}) fusion(f32[6,256,256]{1,2,0:T(8,128)S(1)} %fusion.7, f32[6,256]{1,0:T(8,128)S(1)} %mul.69, bf16[1,128,3584]{2,1,0:T(8,128)(2,1)S(1)} %copy-done.4, ...), kind=kOutput, calls=%fused_computation.39 | convolution fusion | flops 1413478912 | bytes 15609857 | tf_op jit(solution)/shard_map/dot_general | solution.py:243
  358.0 0.7 all_to_all.16
  358.8 6.8 %all-to-all-start = ((f32[8,1,192]{2,1,0:T(1,128)}), f32[8,1,192]{2,1,0:T(1,128)S(1)}, u32[]{:S(2)}, u32[]{:S(2)}) async-start(f32[8,1,192]{2,1,0:T(1,128)} %all_to_all.16), calls=%async_computation | async-start | bytes 16384 | tf_op jit(solution)/shard_map/all_to_all | solution.py:257
  365.6 7.2 %fusion.13 = bf16[3584,256]{1,0:T(8,128)(2,1)S(1)} fusion(bf16[6,256,7296]{2,1,0:T(8,128)(2,1)} %get-tuple-element.8, bf16[6,256,128]{1,2,0:T(8,128)(2,1)S(1)} %get-tuple-element.31, bf16[6,256,128]{1,2,0:T(8,128)(2,1)S(1)} %get-tuple-element.32), kind=kOutput, calls=%fused_computation.12 | convolution fusion | flops 2821062656 | bytes 13631488 | tf_op jit(solution)/shard_map/dot_general | solution.py:252
  372.8 1.3 slice_bitcast_fusion
  374.6 0.7 all_to_all.14
  375.3 15.2 %all-to-all-start.1 = ((f32[32,1,6]{2,1,0:T(1,128)}), f32[32,1,6]{2,1,0:T(1,128)S(1)}, u32[]{:S(2)}, u32[]{:S(2)}) async-start(f32[32,1,6]{2,1,0:T(1,128)} %bitcast.13), calls=%async_computation.1 | async-start | bytes 32768 | tf_op jit(solution)/shard_map/all_to_all | solution.py:259
  390.5 6.2 %fusion.22 = bf16[1,128,3584]{2,1,0:T(8,128)(2,1)} fusion(bf16[6,256,128]{1,2,0:T(8,128)(2,1)S(1)} %get-tuple-element.25, bf16[6,256,7296]{2,1,0:T(8,128)(2,1)} %get-tuple-element.8, bf16[6,256]{1,0:T(8,128)(2,1)S(1)} %slice_reduce_fusion), kind=kOutput, calls=%fused_computation.15 | convolution fusion | flops 1415249920 | bytes 12323840 | tf_op jit(solution)/shard_map/dot_general | solution.py:255
  396.7 1.1 all-to-all-done.1
  398.3 0.7 reduce.7
  399.4 0.7 copy.52
  (35 shorter events, 2.9 us)
Async XLA Ops:
  78.8 3.9 copy-start.3
  82.7 260.9 %copy-start = (bf16[1,3584,128]{2,1,0:T(8,128)(2,1)S(1)}, bf16[1,3584,128]{2,1,0:T(8,128)(2,1)}, u32[]{:S(2)}) copy-start(bf16[1,3584,128]{2,1,0:T(8,128)(2,1)} %wg_ref.1) | copy-start | bytes 2752516
  82.7 260.9 %copy-start.1 = (bf16[1,3584,128]{2,1,0:T(8,128)(2,1)S(1)}, bf16[1,3584,128]{2,1,0:T(8,128)(2,1)}, u32[]{:S(2)}) copy-start(bf16[1,3584,128]{2,1,0:T(8,128)(2,1)} %wu_ref.1) | copy-start | bytes 2752516
  343.9 6.0 %copy-start.2 = (bf16[1,128,3584]{2,1,0:T(8,128)(2,1)S(1)}, bf16[1,128,3584]{2,1,0:T(8,128)(2,1)}, u32[]{:S(2)}) copy-start(bf16[1,128,3584]{2,1,0:T(8,128)(2,1)} %wd_ref.1) | copy-start | bytes 2752516
  343.9 6.0 %copy-start.4 = (bf16[1,128,3584]{2,1,0:T(8,128)(2,1)S(1)}, bf16[1,128,3584]{2,1,0:T(8,128)(2,1)}, u32[]{:S(2)}) copy-start(bf16[1,128,3584]{2,1,0:T(8,128)(2,1)} %get-tuple-element.9) | copy-start | bytes 2752516
  358.8 15.8 %all-to-all-start = ((f32[8,1,192]{2,1,0:T(1,128)}), f32[8,1,192]{2,1,0:T(1,128)S(1)}, u32[]{:S(2)}, u32[]{:S(2)}) async-start(f32[8,1,192]{2,1,0:T(1,128)} %all_to_all.16), calls=%async_computation | async-start | bytes 16384 | tf_op jit(solution)/shard_map/all_to_all | solution.py:257
  375.3 22.5 %all-to-all-start.1 = ((f32[32,1,6]{2,1,0:T(1,128)}), f32[32,1,6]{2,1,0:T(1,128)S(1)}, u32[]{:S(2)}, u32[]{:S(2)}) async-start(f32[32,1,6]{2,1,0:T(1,128)} %bitcast.13), calls=%async_computation.1 | async-start | bytes 32768 | tf_op jit(solution)/shard_map/all_to_all | solution.py:259
where the time goes:
time: 401 us; the launch traced here: 400 us
  Pallas kernels  319 us (80%)
  matrix products  30.4 us (8%)
  local copies, waits for them, and re-layouts  22.3 us (6%)
  starting transfers between devices  22 us (5%)
    pallas_call x1, Pallas kernels, dp_gather(): pl.pallas_call(functools.partial(dp_gather_kernel, n_dp, ring, chunks, n_...  258 us
    pallas_call x1, Pallas kernels, expert_exchange(): pl.pallas_call(functools.partial(expert_exchange_kernel, n_ex), out_shape...  60.9 us
    all_to_all x1, starting transfers between devices, body(): lax.all_to_all(own_scores, 'expert', split_axis=0, concat_axis=0, tiled=T...  15.2 us
    reshape x2, local copies, waits for them, and re-layouts, body(): recv = expert_exchange(packed).reshape(axis_len, CAP, row_width)  10.2 us
  transfers between devices with their start and end apart: 2, of which 2 were waited for; matrix products, arithmetic and copies ran while one was open for 4% of the time, Pallas kernels for 0%

commit v1 on v0

--- a/solution.py
+++ b/solution.py
@@ -51,18 +51,6 @@
 
     local = pltpu.make_async_copy(x_ref, span(me, 0, rows), recv.at[me])
     local.start()
-    swaps = []
-    for index, (src, dst) in enumerate(((wg_ref, og_ref), (wu_ref, ou_ref), (wd_ref, od_ref))):
-        copy = pltpu.make_async_remote_copy(
-            src_ref=src,
-            dst_ref=dst,
-            send_sem=send.at[3 * chunks + 6 + index],
-            recv_sem=recv_w.at[index],
-            device_id=(me, twin),
-            device_id_type=pl.DeviceIdType.MESH,
-        )
-        copy.start()
-        swaps.append(copy)
     sent = []
     for q in range(chunks):
         sent.append(
@@ -85,6 +73,18 @@
         arrived(chunk, recv_z.at[q])
         sent.append(push(chunk, chunk, len(sent), recv.at[across], left))
         sent.append(push(chunk, chunk, len(sent), recv.at[across], right))
+    swaps = []
+    for index, (src, dst) in enumerate(((wg_ref, og_ref), (wu_ref, ou_ref), (wd_ref, od_ref))):
+        copy = pltpu.make_async_remote_copy(
+            src_ref=src,
+            dst_ref=dst,
+            send_sem=send.at[3 * chunks + 6 + index],
+            recv_sem=recv_w.at[index],
+            device_id=(me, twin),
+            device_id_type=pl.DeviceIdType.MESH,
+        )
+        copy.start()
+        swaps.append(copy)
     left_across = (left + ring) % n_dp
     right_across = (right + ring) % n_dp
     arrived(span(left_across, 0, rows), recv.at[left_across])

time: 401 us -> 401 us (level)
  starting transfers between devices: 22 us -> 16.8 us
where the time goes in v1:
time: 401 us; the launch traced here: 400 us
  Pallas kernels  323 us (81%)
  matrix products  30.4 us (8%)
  local copies, waits for them, and re-layouts  22.3 us (6%)
  starting transfers between devices  16.8 us (4%)
  other arithmetic  4.49 us (1%)
    pallas_call x1, Pallas kernels, dp_gather(): pl.pallas_call(functools.partial(dp_gather_kernel, n_dp, ring, chunks, n_...  262 us
    pallas_call x1, Pallas kernels, expert_exchange(): pl.pallas_call(functools.partial(expert_exchange_kernel, n_ex), out_shape...  60.9 us
    all_to_all x1, starting transfers between devices, body(): lax.all_to_all(own_scores, 'expert', split_axis=0, concat_axis=0, tiled=T...  12 us
    reshape x2, local copies, waits for them, and re-layouts, body(): recv = expert_exchange(packed).reshape(axis_len, CAP, row_width)  10.2 us
  transfers between devices with their start and end apart: 2, of which 2 were waited for; matrix products, arithmetic and copies ran while one was open for 4% of the time, Pallas kernels for 0%

profile of v1, /device:TPU:1, one launch (start us, length us, event | category | flops | bytes accessed | tf_op | source)
XLA Modules:
  0.0 400.2 jit_solution(6741555165572765551)
XLA Ops:
  0.7 0.8 copy.44
  1.6 0.8 copy.39
  2.5 0.7 select_reduce_fusion.1
  4.5 2.3 convolution_convert_fusion
  7.0 4.5 %reshape.127.x_ref = bf16[32,342,128]{2,1,0:T(8,128)(2,1)} reshape(bf16[192,7296]{1,0:T(8,128)(2,1)S(1)} %pad_maximum_fusion) | data formatting | bytes 5603328 | tf_op jit(solution)/shard_map/reshape | solution.py:221
  11.5 60.9 %shard_map.111 = bf16[32,342,128]{2,1,0:T(8,128)(2,1)} custom-call(bf16[32,342,128]{2,1,0:T(8,128)(2,1)} %reshape.127.x_ref), custom_call_target="tpu_custom_call" | custom-call | tf_op jit(solution)/shard_map/pallas_call | solution.py:165
  72.5 6.3 %reshape.128 = bf16[32,6,7296]{2,1,0:T(8,128)(2,1)} reshape(bf16[32,342,128]{2,1,0:T(8,128)(2,1)} %shard_map.111) | data formatting | bytes 5603328 | tf_op jit(solution)/shard_map/reshape | solution.py:222
  78.8 3.9 copy.58
  82.7 0.6 fusion.56
  83.3 262.2 %shard_map.112 = (bf16[6,256,7296]{2,1,0:T(8,128)(2,1)}, bf16[1,3584,128]{2,1,0:T(8,128)(2,1)}, bf16[1,3584,128]{2,1,0:T(8,128)(2,1)}, bf16[1,128,3584]{2,1,0:T(8,128)(2,1)}) custom-call(bf16[6,32,7296]{2,1,0:T(8,128)(2,1)} %bitcast.38, bf16[1,3584,128]{2,1,0:T(8,128)(2,1)} %wg_ref.1, bf16[1,3584,128]{2,1,0:T(8,128)(2,1)} %wu_ref.1, bf16[1,128,3584]{2,1,0:T(8,128)(2,1)} %wd_ref.1), custom_call_target="tpu_custom_call" | custom-call | tf_op jit(solution)/shard_map/pallas_call | solution.py:116
  345.5 1.2 slice_reduce_fusion
  347.4 1.8 select_bitcast_fusion
  349.2 6.0 %fusion.7 = f32[6,256,256]{1,2,0:T(8,128)S(1)} fusion(bf16[6,256,7296]{2,1,0:T(8,128)(2,1)} %get-tuple-element.8, bf16[3584,128]{1,0:T(8,128)(2,1)S(1)} %get-tuple-element.37, bf16[3584,128]{1,0:T(8,128)(2,1)S(1)} %get-tuple-element.38), kind=kOutput, calls=%fused_computation.7 | convolution fusion | flops 2822242304 | bytes 14417920 | tf_op jit(solution)/shard_map/dot_general | solution.py:237
  355.2 7.9 %multiply_reduce_fusion = (f32[6,256]{1,0:T(8,128)S(1)}, bf16[6,256,128]{1,2,0:T(8,128)(2,1)S(1)}, bf16[6,256,128]{1,2,0:T(8,128)(2,1)S(1)}, bf16[6,256,128]{1,2,0:T(8,128)(2,1)S(1)}) fusion(f32[6,256,256]{1,2,0:T(8,128)S(1)} %fusion.7, f32[6,256]{1,0:T(8,128)S(1)} %mul.69, bf16[1,128,3584]{2,1,0:T(8,128)(2,1)S(1)} %copy-done.4, ...), kind=kOutput, calls=%fused_computation.39 | convolution fusion | flops 1413478912 | bytes 15609857 | tf_op jit(solution)/shard_map/dot_general | solution.py:243
  363.3 0.7 all_to_all.16
  364.0 4.8 %all-to-all-start = ((f32[8,1,192]{2,1,0:T(1,128)}), f32[8,1,192]{2,1,0:T(1,128)S(1)}, u32[]{:S(2)}, u32[]{:S(2)}) async-start(f32[8,1,192]{2,1,0:T(1,128)} %all_to_all.16), calls=%async_computation | async-start | bytes 16384 | tf_op jit(solution)/shard_map/all_to_all | solution.py:257
  368.8 7.2 %fusion.13 = bf16[3584,256]{1,0:T(8,128)(2,1)S(1)} fusion(bf16[6,256,7296]{2,1,0:T(8,128)(2,1)} %get-tuple-element.8, bf16[6,256,128]{1,2,0:T(8,128)(2,1)S(1)} %get-tuple-element.31, bf16[6,256,128]{1,2,0:T(8,128)(2,1)S(1)} %get-tuple-element.32), kind=kOutput, calls=%fused_computation.12 | convolution fusion | flops 2821062656 | bytes 13631488 | tf_op jit(solution)/shard_map/dot_general | solution.py:252
  376.0 1.3 slice_bitcast_fusion
  377.9 0.7 all_to_all.14
  378.6 12.0 %all-to-all-start.1 = ((f32[32,1,6]{2,1,0:T(1,128)}), f32[32,1,6]{2,1,0:T(1,128)S(1)}, u32[]{:S(2)}, u32[]{:S(2)}) async-start(f32[32,1,6]{2,1,0:T(1,128)} %bitcast.13), calls=%async_computation.1 | async-start | bytes 32768 | tf_op jit(solution)/shard_map/all_to_all | solution.py:259
  390.6 6.2 %fusion.22 = bf16[1,128,3584]{2,1,0:T(8,128)(2,1)} fusion(bf16[6,256,128]{1,2,0:T(8,128)(2,1)S(1)} %get-tuple-element.25, bf16[6,256,7296]{2,1,0:T(8,128)(2,1)} %get-tuple-element.8, bf16[6,256]{1,0:T(8,128)(2,1)S(1)} %slice_reduce_fusion), kind=kOutput, calls=%fused_computation.15 | convolution fusion | flops 1415249920 | bytes 12323840 | tf_op jit(solution)/shard_map/dot_general | solution.py:255
  396.8 1.1 all-to-all-done.1
  398.4 0.7 reduce.7
  399.5 0.7 copy.52
  (35 shorter events, 3.2 us)
Async XLA Ops:
  78.8 3.9 copy-start.3
  82.7 264.7 %copy-start = (bf16[1,3584,128]{2,1,0:T(8,128)(2,1)S(1)}, bf16[1,3584,128]{2,1,0:T(8,128)(2,1)}, u32[]{:S(2)}) copy-start(bf16[1,3584,128]{2,1,0:T(8,128)(2,1)} %wg_ref.1) | copy-start | bytes 2752516
  82.7 264.7 %copy-start.1 = (bf16[1,3584,128]{2,1,0:T(8,128)(2,1)S(1)}, bf16[1,3584,128]{2,1,0:T(8,128)(2,1)}, u32[]{:S(2)}) copy-start(bf16[1,3584,128]{2,1,0:T(8,128)(2,1)} %wu_ref.1) | copy-start | bytes 2752516
  349.1 6.0 %copy-start.2 = (bf16[1,128,3584]{2,1,0:T(8,128)(2,1)S(1)}, bf16[1,128,3584]{2,1,0:T(8,128)(2,1)}, u32[]{:S(2)}) copy-start(bf16[1,128,3584]{2,1,0:T(8,128)(2,1)} %wd_ref.1) | copy-start | bytes 2752516
  349.2 6.0 %copy-start.4 = (bf16[1,128,3584]{2,1,0:T(8,128)(2,1)S(1)}, bf16[1,128,3584]{2,1,0:T(8,128)(2,1)}, u32[]{:S(2)}) copy-start(bf16[1,128,3584]{2,1,0:T(8,128)(2,1)} %get-tuple-element.9) | copy-start | bytes 2752516
  364.0 13.8 %all-to-all-start = ((f32[8,1,192]{2,1,0:T(1,128)}), f32[8,1,192]{2,1,0:T(1,128)S(1)}, u32[]{:S(2)}, u32[]{:S(2)}) async-start(f32[8,1,192]{2,1,0:T(1,128)} %all_to_all.16), calls=%async_computation | async-start | bytes 16384 | tf_op jit(solution)/shard_map/all_to_all | solution.py:257
  378.6 19.3 %all-to-all-start.1 = ((f32[32,1,6]{2,1,0:T(1,128)}), f32[32,1,6]{2,1,0:T(1,128)S(1)}, u32[]{:S(2)}, u32[]{:S(2)}) async-start(f32[32,1,6]{2,1,0:T(1,128)} %bitcast.13), calls=%async_computation.1 | async-start | bytes 32768 | tf_op jit(solution)/shard_map/all_to_all | solution.py:259
